TPU v7x, 256 devices: a whole 4x4x8 slice. The times are simulated.
256 devices in a mesh: row: 16 (over z, x_lo), col: 8 (over x_hi, y), depth: 2 (over core).
Axes of the slice: x: 4 (x_hi: 2, x_lo: 2; x = x_hi * 2 + x_lo), y: 4, z: 8, core: 2. Of those that a mesh axis runs over, the one named last changes fastest.
Arguments:
- row_slab: bfloat16 [2048, 53248], P('row', ('col', 'depth')), may hold values from -6 to 6
- col_slab: bfloat16 [53248, 4096], P('row', ('col', 'depth')), may hold values from -0.046875 to 0.046875
- row_occupied: int32 [16, 416], P('row', ('col', 'depth')), may hold values 0 or 1
- col_occupied: int32 [416, 32], P('row', ('col', 'depth')), may hold values 0 or 1
- keep_mask: int32 [16, 32], P('row', ('col', 'depth')), may hold values 0 or 1
Outputs:
- squared: bfloat16 [2048, 4096], P('row', ('col', 'depth'))
All inputs are finite; a program needn't handle non-finite values. No bound on the sum of `row_occupied` or of `col_occupied` or of `keep_mask` on one device may be relied on, other than what follows from the above.
Results may differ from a plain program's by a relative error of at most 0.001.
Values may be sent and summed in bfloat16 or wider, within the bound.
No kernel may reach another device: no remote copies, remote signals or barrier semaphores. Data moves between devices by JAX's collectives and lax.ppermute only.
A program may use at most 192 MiB of HBM per device.

v0:
```python
import jax
import jax.numpy as jnp
from jax import lax
from jax.sharding import PartitionSpec as P

BLK = 128


def masked(matrix, occupied):
    row_count = matrix.shape[0] // BLK
    col_count = matrix.shape[1] // BLK
    blocks = (
        matrix.reshape(row_count, BLK, col_count, BLK)
        * occupied.astype(matrix.dtype)[:, None, :, None]
    )
    return blocks.reshape(matrix.shape)


def local(row_slab, col_slab, row_occupied, col_occupied, keep_mask):
    whole_rows, whole_row_occ = (
        lax.all_gather(row_slab, ("col", "depth"), axis=1, tiled=True),
        lax.all_gather(row_occupied, ("col", "depth"), axis=1, tiled=True),
    )
    left_band = masked(whole_rows, whole_row_occ)
    segment = masked(
        lax.all_gather(col_slab, "row", axis=0, tiled=True),
        lax.all_gather(col_occupied, "row", axis=0, tiled=True),
    )
    product = jnp.dot(left_band, segment, preferred_element_type=jnp.float32)
    return masked(product, keep_mask).astype(jnp.bfloat16)


def solution(mesh):
    placed = (
        P("row", ("col", "depth")),
        P("row", ("col", "depth")),
        P("row", ("col", "depth")),
        P("row", ("col", "depth")),
        P("row", ("col", "depth")),
    )
    return jax.shard_map(
        local, mesh=mesh, in_specs=placed, out_specs=P("row", ("col", "depth")), check_vma=False
    )
```

profile of v0, /device:TPU:1, one launch (start us, length us, event | category | flops | bytes accessed | tf_op | source)
XLA Modules:
  0.0 702.5 jit_solution(5745444827072541923)
XLA Ops:
  6.5 0.0 all-gather.6.cloned.1.call-start
  6.5 0.7 all-gather.6.cloned.1.call-update
  7.3 0.0 all-gather.4.cloned.1.call-start
  7.3 0.7 all-gather.4.cloned.1.call-update
  8.0 45.2 %all-gather = s32[16,26,2]{1,2,0:T(2,128)S(1)} all-gather(s32[1,26,2]{1,2,0:T(2,128)} %bitcast.31), channel_id=1, replica_groups=mesh['row'=16,'col'=8,'depth'=2] {'row'}, dimensions={0}, use_global_device_ids=true | all-gather | bytes 3536 | tf_op jit(solution)/shard_map/all_gather | solution.py:27
  53.2 0.1 reshape.29
  53.3 0.2 copy.13
  53.5 1.3 dynamic-slice
  55.4 0.8 bitcast_dynamic-update-slice_fusion
  56.2 22.9 %all-reduce = s32[416]{0:T(512)S(1)} all-reduce(s32[416]{0:T(512)S(1)} %bitcast_dynamic-update-slice_fusion), channel_id=1, replica_groups=mesh['row'=16,'col'=8,'depth'=2] {'col','depth'}, use_global_device_ids=true, to_apply=%add | all-reduce | flops 416 | bytes 3328
  79.1 0.7 convert_bitcast_fusion
  79.8 0.1 broadcast_bitcast_fusion
  79.9 494.8 %all-gather.6.cloned.1.call-done = bf16[53248,256]{1,0:T(8,128)(2,1)} async-done(((bf16[3328,256]{1,0:T(8,128)(2,1)}), bf16[53248,256]{1,0:T(8,128)(2,1)}) %all-gather.6.cloned.1.call-update) | async-done | bytes 27262992 | tf_op jit(solution)/shard_map/all_gather | solution.py:26
  574.7 19.1 %mul.44 = bf16[416,128,2,128]{3,2,1,0:T(2,128)(2,1)} broadcast(bf16[416,2]{1,0:T(8,128)(2,1)S(1)} %copy.13), dimensions={0,2} | broadcast | bytes 27264640 | tf_op jit(solution)/shard_map/mul | solution.py:13
  593.8 27.7 %fusion = bf16[256,53248]{0,1:T(8,128)(2,1)} fusion(bf16[53248,256]{1,0:T(8,128)(2,1)} %all-gather.6.cloned.1.call-done, bf16[6656,8,2,128]{3,2,1,0:T(2,128)(2,1)} %bitcast.28), kind=kLoop, calls=%fused_computation.1 | loop fusion | flops 13631488 | bytes 81788928 | tf_op jit(solution)/shard_map/dot_general | solution.py:29
  621.5 32.5 %copy.16 = bf16[256,53248]{1,0:T(8,128)(2,1)} copy(bf16[256,53248]{0,1:T(8,128)(2,1)} %fusion) | data formatting | bytes 54525952 | tf_op jit(solution)/shard_map/dot_general | solution.py:29
  654.0 24.6 %all-gather.4.cloned.1.call-done = bf16[128,53248]{1,0:T(8,128)(2,1)} async-done(((bf16[128,3328]{1,0:T(8,128)(2,1)}), bf16[128,53248]{1,0:T(8,128)(2,1)}) %all-gather.4.cloned.1.call-update) | async-done | bytes 13631504 | tf_op jit(solution)/shard_map/all_gather | solution.py:21
  678.6 16.4 %fusion.8 = bf16[128,2,128]{0,2,1:T(8,128)(2,1)S(1)} fusion(bf16[2,128,53248]{2,1,0:T(8,128)(2,1)} %bitcast.29, bf16[128,53248]{1,0:T(8,128)(2,1)} %all-gather.4.cloned.1.call-done, bf16[53248]{0:T(1024)(128)(2,1)S(1)} %broadcast_bitcast_fusion, f32[2]{0:T(128)S(1)} %convert_bitcast_fusion), kind=kOutput, calls=%fused_computation.7 | convolution fusion | flops 3516989440 | bytes 41066504 | tf_op jit(solution)/shard_map/dot_general | solution.py:29
  695.0 0.7 copy.15
  (4 shorter events, 0.0 us)
Async XLA Ops:
  6.5 568.1 %all-gather.6.cloned.1.call-start = ((), (), s32[]{:S(2)}) async-start(), calls=%async_computation.1 | async-start | bytes 28966912 | tf_op jit(solution)/shard_map/all_gather | solution.py:26
  7.3 671.3 %all-gather.4.cloned.1.call-start = ((), (), s32[]{:S(2)}) async-start(), calls=%async_computation | async-start | bytes 14483456 | tf_op jit(solution)/shard_map/all_gather | solution.py:21
Sparse Core Ops, SparseCore 0:
  9.1 565.4 all-gather.5
  577.4 101.1 all-gather.3
where the time goes:
time: 704 us; the launch traced here: 703 us
  waiting for transfers between devices  521 us (74%)
  blocking collectives  68.1 us (10%)
  local copies, waits for them, and re-layouts  54.8 us (8%)
  other arithmetic  28.4 us (4%)
  matrix products  16.4 us (2%)
  between operations  14.1 us (2%)
    all_gather x1, waiting for transfers between devices, local(): lax.all_gather(col_slab, 'row', axis=0, tiled=True)  495 us
    all_gather x1, blocking collectives, local(): lax.all_gather(col_occupied, 'row', axis=0, tiled=True)  45.2 us
    dot_general x1, local copies, waits for them, and re-layouts, local(): product = jnp.dot(left_band, segment, preferred_element_type=jnp.float32)  32.5 us
    dot_general x1, other arithmetic, local(): product = jnp.dot(left_band, segment, preferred_element_type=jnp.float32)  27.7 us
    all_gather x1, waiting for transfers between devices, local(): lax.all_gather(row_slab, ('col', 'depth'), axis=1, tiled=True)  24.6 us
    unnamed x1, blocking collectives  22.9 us
    mul x2, local copies, waits for them, and re-layouts, masked(): matrix.reshape(row_count, BLK, col_count, BLK)  19.3 us
    dot_general x1, matrix products, local(): product = jnp.dot(left_band, segment, preferred_element_type=jnp.float32)  16.4 us
  transfers between devices with their start and end apart: 2, of which 2 were waited for; matrix products, arithmetic and copies ran while one was open for 12% of the time, Pallas kernels for 0%

commit v1 on v0

--- a/solution.py
+++ b/solution.py
@@ -4,6 +4,15 @@
 from jax.sharding import PartitionSpec as P
 
 BLK = 128
+remake_spot = lambda xx, shard_axis, dimension_no: jnp.concatenate(
+    lax.all_to_all(
+        jnp.stack(lax.axis_size(shard_axis) * [xx], 0),
+        axis_name=shard_axis,
+        split_axis=0,
+        concat_axis=0,
+    ),
+    dimension_no,
+)
 
 
 def masked(matrix, occupied):
@@ -23,8 +32,7 @@
     )
     left_band = masked(whole_rows, whole_row_occ)
     segment = masked(
-        lax.all_gather(col_slab, "row", axis=0, tiled=True),
-        lax.all_gather(col_occupied, "row", axis=0, tiled=True),
+        remake_spot(col_slab, "row", 0), lax.all_gather(col_occupied, "row", axis=0, tiled=True)
     )
     product = jnp.dot(left_band, segment, preferred_element_type=jnp.float32)
     return masked(product, keep_mask).astype(jnp.bfloat16)

time: 704 us -> 825 us (1.17)
  blocking collectives: 68.1 us -> 654 us
  waiting for transfers between devices: 521 us -> 0.69 us
  local copies, waits for them, and re-layouts: 54.8 us -> 99.5 us
  starting transfers between devices: 0.04 us -> 10.3 us
    all_gather x1, blocking collectives: 45.2 us -> 637 us  [local(): lax.all_gather(col_occupied, 'row', axis=0, tiled=True)]
    all_gather x1 -> x0, waiting for transfers between devices: 495 us -> none  [local(): lax.all_gather(col_slab, 'row', axis=0, tiled=True)]
    all_to_all x0 -> x1, local copies, waits for them, and re-layouts: none -> 33.3 us  [lax.all_to_all(jnp.stack(lax.axis_size(shard_axis) * [xx], 0), axis_name=...]
    all_gather x1, waiting for transfers between devices: 24.6 us -> 0.01 us  [local(): lax.all_gather(row_slab, ('col', 'depth'), axis=1, tiled=True)]
    all_to_all x0 -> x1, starting transfers between devices: none -> 10.2 us  [lax.all_to_all(jnp.stack(lax.axis_size(shard_axis) * [xx], 0), axis_name=...]
    another operation x0 -> x1, local copies, waits for them, and re-layouts: none -> 9.39 us  [jnp.stack(lax.axis_size(shard_axis) * [xx], 0)]
  transfers between devices with their start and end apart: 2 -> 2, of which waited for: 2 -> 0; matrix products, arithmetic and copies ran while one was open for 12% -> 14% of each run, Pallas kernels for 0% -> 0%
where the time goes in v1:
time: 825 us; the launch traced here: 823 us
  blocking collectives  654 us (79%)
  local copies, waits for them, and re-layouts  99.5 us (12%)
  other arithmetic  27.7 us (3%)
  matrix products  16.5 us (2%)
  between operations  14.2 us (2%)
  starting transfers between devices  10.3 us (1%)
    all_gather x1, blocking collectives, local(): lax.all_gather(col_occupied, 'row', axis=0, tiled=True)  637 us
    all_to_all x1, local copies, waits for them, and re-layouts, lax.all_to_all(jnp.stack(lax.axis_size(shard_axis) * [xx], 0), axis_name=...  33.3 us
    dot_general x1, local copies, waits for them, and re-layouts, local(): product = jnp.dot(left_band, segment, preferred_element_type=jnp.float32)  33 us
    dot_general x1, other arithmetic, local(): product = jnp.dot(left_band, segment, preferred_element_type=jnp.float32)  27.6 us
    mul x2, local copies, waits for them, and re-layouts, masked(): matrix.reshape(row_count, BLK, col_count, BLK)  19.3 us
    unnamed x1, blocking collectives  17.3 us
    dot_general x1, matrix products, local(): product = jnp.dot(left_band, segment, preferred_element_type=jnp.float32)  16.5 us
  transfers between devices with their start and end apart: 2, of which 0 were waited for; matrix products, arithmetic and copies ran while one was open for 14% of the time, Pallas kernels for 0%

profile of v1, /device:TPU:1, one launch (start us, length us, event | category | flops | bytes accessed | tf_op | source)
XLA Modules:
  0.0 822.8 jit_solution(12006194050198091246)
XLA Ops:
  6.5 2.7 copy.14
  9.3 9.4 %stack.2 = bf16[16,3328,256]{1,2,0:T(8,128)(2,1)} broadcast(bf16[3328,256]{0,1:T(8,128)(2,1)S(1)} %copy.14), dimensions={1,2} | broadcast | bytes 28966912 | tf_op jit(solution)/shard_map/stack | solution.py:9
  18.7 0.0 copy-start
  18.7 0.0 copy-start.3
  18.7 0.0 copy-start.1
  18.7 0.0 copy-start.2
  18.7 10.2 %all-to-all-start = ((bf16[16,3328,256]{1,2,0:T(8,128)(2,1)}), bf16[16,3328,256]{1,2,0:T(8,128)(2,1)}, u32[]{:S(2)}, u32[]{:S(2)}) async-start(bf16[16,3328,256]{1,2,0:T(8,128)(2,1)} %stack.2), calls=%async_computation | async-start | bytes 54525952 | tf_op jit(solution)/shard_map/all_to_all | solution.py:8
  28.9 0.0 all-gather.3.cloned.1.call-start
  29.0 0.7 all-gather.3.cloned.1.call-update
  29.7 0.0 copy-done
  29.7 636.7 %all-gather = s32[16,26,2]{1,2,0:T(2,128)S(1)} all-gather(s32[1,26,2]{1,2,0:T(2,128)S(1)} %bitcast.33), channel_id=1, replica_groups=mesh['row'=16,'col'=8,'depth'=2] {'row'}, dimensions={0}, use_global_device_ids=true | all-gather | bytes 3536 | tf_op jit(solution)/shard_map/all_gather | solution.py:35
  666.4 0.1 reshape.31
  666.5 0.2 copy.17
  666.7 0.0 copy-done.3
  666.7 0.6 dynamic-slice
  668.0 0.0 copy-done.1
  668.0 0.1 bitcast_dynamic-update-slice_fusion
  668.1 17.3 %all-reduce = s32[416]{0:T(512)S(1)} all-reduce(s32[416]{0:T(512)S(1)} %bitcast_dynamic-update-slice_fusion), channel_id=1, replica_groups=mesh['row'=16,'col'=8,'depth'=2] {'col','depth'}, use_global_device_ids=true, to_apply=%add | all-reduce | flops 416 | bytes 3328
  685.4 0.0 copy-done.2
  685.4 0.1 broadcast_bitcast_fusion
  685.5 0.0 all-to-all-done
  685.5 33.3 %copy.15 = bf16[16,3328,256]{2,1,0:T(8,128)(2,1)} copy(bf16[16,3328,256]{1,2,0:T(8,128)(2,1)} %all-to-all-done) | data formatting | bytes 54525952 | tf_op jit(solution)/shard_map/all_to_all | solution.py:8
  718.9 19.1 %mul.44 = bf16[416,128,2,128]{3,2,1,0:T(2,128)(2,1)} broadcast(bf16[416,2]{1,0:T(8,128)(2,1)S(1)} %copy.17), dimensions={0,2} | broadcast | bytes 27264640 | tf_op jit(solution)/shard_map/mul | solution.py:22
  738.0 27.6 %fusion = bf16[256,53248]{0,1:T(8,128)(2,1)} fusion(bf16[6656,8,2,128]{3,2,1,0:T(2,128)(2,1)} %bitcast.30, bf16[16,3328,256]{2,1,0:T(8,128)(2,1)} %copy.15), kind=kLoop, calls=%fused_computation.1 | loop fusion | flops 13631488 | bytes 81788928 | tf_op jit(solution)/shard_map/dot_general | solution.py:37
  765.6 33.0 %copy.20 = bf16[256,53248]{1,0:T(8,128)(2,1)} copy(bf16[256,53248]{0,1:T(8,128)(2,1)} %fusion) | data formatting | bytes 54525952 | tf_op jit(solution)/shard_map/dot_general | solution.py:37
  798.7 0.0 all-gather.3.cloned.1.call-done
  798.7 16.5 %fusion.8 = bf16[128,2,128]{0,2,1:T(8,128)(2,1)S(1)} fusion(bf16[2,128,53248]{2,1,0:T(8,128)(2,1)} %bitcast.31, bf16[128,53248]{1,0:T(8,128)(2,1)} %all-gather.3.cloned.1.call-done, bf16[53248]{0:T(1024)(128)(2,1)S(1)} %broadcast_bitcast_fusion, f32[2]{0:T(128)S(1)} %convert_bitcast_fusion), kind=kOutput, calls=%fused_computation.7 | convolution fusion | flops 3516989440 | bytes 41066504 | tf_op jit(solution)/shard_map/dot_general | solution.py:37
  815.2 0.7 copy.19
  (5 shorter events, 0.0 us)
Async XLA Ops:
  18.7 11.0 %copy-start = (s32[26,2]{0,1:T(2,128)S(1)}, s32[26,2]{0,1:T(2,128)}, u32[]{:S(2)}) copy-start(s32[26,2]{0,1:T(2,128)} %param.8) | copy-start | bytes 628
  18.7 648.0 %copy-start.3 = (u32[256]{0:T(256)S(1)}, u32[256]{0:T(256)}, u32[]{:S(2)}) copy-start(u32[256]{0:T(256)} %constant.5) | copy-start | bytes 3076
  18.7 649.3 %copy-start.1 = (s32[1,26]{1,0:T(1,128)S(1)}, s32[1,26]{1,0:T(1,128)}, u32[]{:S(2)}) copy-start(s32[1,26]{1,0:T(1,128)} %param.7) | copy-start | bytes 316
  18.7 666.7 %copy-start.2 = (s32[1,2]{1,0:T(1,128)S(1)}, s32[1,2]{1,0:T(1,128)}, u32[]{:S(2)}) copy-start(s32[1,2]{1,0:T(1,128)} %param.9) | copy-start | bytes 28
  18.7 666.9 %all-to-all-start = ((bf16[16,3328,256]{1,2,0:T(8,128)(2,1)}), bf16[16,3328,256]{1,2,0:T(8,128)(2,1)}, u32[]{:S(2)}, u32[]{:S(2)}) async-start(bf16[16,3328,256]{1,2,0:T(8,128)(2,1)} %stack.2), calls=%async_computation | async-start | bytes 54525952 | tf_op jit(solution)/shard_map/all_to_all | solution.py:8
  28.9 769.8 %all-gather.3.cloned.1.call-start = ((), (), s32[]{:S(2)}) async-start(), calls=%async_computation.1 | async-start | bytes 14483456 | tf_op jit(solution)/shard_map/all_gather | solution.py:30
Sparse Core Ops, SparseCore 0:
  32.5 110.8 all-gather.2
